TPU v7x, 32 devices: a whole 2x2x4 slice. The times are simulated.
32 devices in a mesh: dp: 8 (over z, x), tensor: 4 (over y, core).
Axes of the slice: x: 2, y: 2, z: 4, core: 2. Of those that a mesh axis runs over, the one named last changes fastest.
Arguments:
- hidden_in: float32 [4096, 1536], P('dp'), may hold values from -6 to 6
- doc_lengths: int32 [2, 2], replicated, may hold values from 1 to 1792, 2048 in all within a row
- norm_attn: float32 [2, 1536], replicated, may hold values from 0.5 to 1.5
- norm_mlp: float32 [2, 1536], replicated, may hold values from 0.5 to 1.5
- w_query: bfloat16 [2, 1536, 1536], P(None, None, 'tensor'), may hold values from -0.15625 to 0.15625
- w_key: bfloat16 [2, 1536, 768], P(None, None, 'tensor'), may hold values from -0.15625 to 0.15625
- w_value: bfloat16 [2, 1536, 768], P(None, None, 'tensor'), may hold values from -0.15625 to 0.15625
- w_out: bfloat16 [2, 1536, 1536], P(None, 'tensor'), may hold values from -0.625 to 0.625
- w_gate: bfloat16 [2, 1536, 4096], P(None, None, 'tensor'), may hold values from -0.15625 to 0.15625
- w_up: bfloat16 [2, 1536, 4096], P(None, None, 'tensor'), may hold values from -0.15625 to 0.15625
- w_down: bfloat16 [2, 4096, 1536], P(None, 'tensor'), may hold values from -0.09375 to 0.09375
- cotangent: float32 [4096, 1536], P('dp'), may hold values from -6 to 6
Outputs:
- hidden_out: float32 [4096, 1536], P('dp')
- input_grad: float32 [4096, 1536], P('dp')
- norm_attn_grad: float32 [2, 1536], P(None, 'dp')
- norm_mlp_grad: float32 [2, 1536], P(None, 'dp')
- w_query_grad: float32 [2, 1536, 1536], P(None, 'dp', 'tensor')
- w_key_grad: float32 [2, 1536, 768], P(None, 'dp', 'tensor')
- w_value_grad: float32 [2, 1536, 768], P(None, 'dp', 'tensor')
- w_out_grad: float32 [2, 1536, 1536], P(None, 'tensor', 'dp')
- w_gate_grad: float32 [2, 1536, 4096], P(None, 'dp', 'tensor')
- w_up_grad: float32 [2, 1536, 4096], P(None, 'dp', 'tensor')
- w_down_grad: float32 [2, 4096, 1536], P(None, 'tensor', 'dp')
Inputs may be any that keep to these rules, and one draw needn't show every extreme that they name: `doc_lengths`: each row holds 2 document lengths that add up to 2048, each at most 1792.
All inputs are finite; a program needn't handle non-finite values.
Results may differ from a plain program's by a relative error of at most 0.028.
Values may be sent and summed in bfloat16 or wider, within the bound.
No kernel may reach another device: no remote copies, remote signals or barrier semaphores. Data moves between devices by JAX's collectives and lax.ppermute only.
A program may use at most 320 MiB of HBM per device.

v0:
```python
import jax
import jax.numpy as jnp
from jax import lax
from jax.sharding import PartitionSpec as P

HD = 96
LAYERS = 2
STRETCHES = 4
EPS = 1e-05
BASE = 100000.0


def passed_along(block, axis, distance):
    devices = range(lax.axis_size(axis))
    route = [((i - distance) % len(devices), i) for i in devices]
    return lax.ppermute(block, axis, route)


def rope_tables(positions):
    half_dim = HD // 2
    frequency = BASE ** (-(jnp.arange(half_dim, dtype=jnp.float32) * 2.0 / HD))
    angles = positions.astype(jnp.float32)[:, None] * frequency[None, :]
    angles = jnp.concatenate([angles, angles], axis=1)
    return (jnp.cos(angles)[:, None, :], jnp.sin(angles)[:, None, :])


def rotate(values, cosine, sine_table):
    half_dim = values.shape[-1] // 2
    turned = jnp.concatenate([-values[..., half_dim:], values[..., :half_dim]], axis=-1)
    return values * cosine + turned * sine_table


def unrotate(gradient, cosine, sine_table):
    half_dim = gradient.shape[-1] // 2
    scaled_values = gradient * sine_table
    turned = jnp.concatenate(
        [scaled_values[..., half_dim:], -scaled_values[..., :half_dim]], axis=-1
    )
    return gradient * cosine + turned


def doc_place(places, lengths):
    doc_ends = jnp.cumsum(lengths, axis=1)
    passed = (places[:, None] >= doc_ends).astype(jnp.int32)
    doc_ids = jnp.sum(passed, axis=1)
    starts = jnp.sum(passed * lengths, axis=1)
    return (doc_ids, places - starts)


def scores_of(queries, key_rows, allowed):
    scores = jnp.einsum(
        "qkgd,tkd->kgqt", queries, key_rows, preferred_element_type=jnp.float32
    ) * HD ** (-0.5)
    return jnp.where(allowed[None, None], scores, -jnp.inf)


def attention_forward(queries, key_rows, value_rows, allowed):
    scores = scores_of(queries, key_rows, allowed)
    row_top = jnp.max(scores, axis=-1, keepdims=True)
    log_total = row_top + jnp.log(jnp.sum(jnp.exp(scores - row_top), axis=-1, keepdims=True))
    attn_probs = jnp.exp(scores - log_total).astype(jnp.bfloat16)
    mixed_heads = jnp.einsum(
        "kgqt,tkd->qkgd", attn_probs, value_rows, preferred_element_type=jnp.float32
    )
    return (mixed_heads.astype(jnp.bfloat16), log_total)


def attention_backward(queries, key_rows, value_rows, allowed, log_total, mixed_grad):
    scores = scores_of(queries, key_rows, allowed)
    attn_probs = jnp.exp(scores - log_total)
    prob_grad = jnp.einsum(
        "qkgd,tkd->kgqt", mixed_grad, value_rows, preferred_element_type=jnp.float32
    )
    centre = jnp.sum(attn_probs * prob_grad, axis=-1, keepdims=True)
    score_grad = (attn_probs * (prob_grad - centre) * HD ** (-0.5)).astype(jnp.bfloat16)
    probs_bf = attn_probs.astype(jnp.bfloat16)
    value_grad = jnp.einsum(
        "kgqt,qkgd->tkd", probs_bf, mixed_grad, preferred_element_type=jnp.float32
    )
    query_grad = jnp.einsum(
        "kgqt,tkd->qkgd", score_grad, key_rows, preferred_element_type=jnp.float32
    )
    key_grad = jnp.einsum("kgqt,qkgd->tkd", score_grad, queries, preferred_element_type=jnp.float32)
    return (query_grad, key_grad, value_grad)


def norm_back(residual_stream, inverse_norm, gain, normalized_gradient, incoming_gradient):
    normalized_input = residual_stream * inverse_norm
    scaled_values = normalized_gradient * gain
    gain_gradient = jnp.sum(normalized_gradient * normalized_input, axis=0)
    residual_gradient = incoming_gradient + inverse_norm * (
        scaled_values
        - normalized_input * jnp.mean(scaled_values * normalized_input, axis=1, keepdims=True)
    )
    return (residual_gradient, gain_gradient)


def forward_layer(residual_stream, params, tables, allowed):
    gain_attn, gain_mlp, query_w, key_w, value_w, out_w, gate_w, up_w, down_w = params
    cosine, sine_table = tables
    row_count = residual_stream.shape[0]
    query_heads = query_w.shape[1] // HD
    kv_heads = key_w.shape[1] // HD
    inv_attn = lax.rsqrt(jnp.mean(residual_stream * residual_stream, axis=1, keepdims=True) + EPS)
    normed_attn = (residual_stream * inv_attn * gain_attn).astype(jnp.bfloat16)
    queries = jnp.dot(normed_attn, query_w, preferred_element_type=jnp.float32).reshape(
        row_count, query_heads, HD
    )
    queries = rotate(queries, cosine, sine_table).astype(jnp.bfloat16)
    key_rows = jnp.dot(normed_attn, key_w, preferred_element_type=jnp.float32).reshape(
        row_count, kv_heads, HD
    )
    key_rows = (
        rotate(key_rows, cosine, sine_table).astype(jnp.bfloat16).reshape(row_count, kv_heads * HD)
    )
    value_rows = jnp.dot(normed_attn, value_w, preferred_element_type=jnp.float32).astype(
        jnp.bfloat16
    )
    key_list = [key_rows]
    value_list = [value_rows]
    for distance in range(1, STRETCHES):
        moved_keys, moved_values = passed_along((key_rows, value_rows), "dp", distance)
        key_list.append(moved_keys)
        value_list.append(moved_values)
    all_keys = jnp.concatenate(key_list, axis=0).reshape(STRETCHES * row_count, kv_heads, HD)
    all_values = jnp.concatenate(value_list, axis=0).reshape(STRETCHES * row_count, kv_heads, HD)
    grouped = queries.reshape(row_count, kv_heads, query_heads // kv_heads, HD)
    mixed_heads, log_total = attention_forward(grouped, all_keys, all_values, allowed)
    mixed_heads = mixed_heads.reshape(row_count, query_heads * HD)
    head_part = jnp.dot(mixed_heads, out_w, preferred_element_type=jnp.float32)
    middle = residual_stream + lax.psum(head_part, "tensor")
    inv_mlp = lax.rsqrt(jnp.mean(middle * middle, axis=1, keepdims=True) + EPS)
    normed_mlp = (middle * inv_mlp * gain_mlp).astype(jnp.bfloat16)
    gate_pre = jnp.dot(normed_mlp, gate_w, preferred_element_type=jnp.float32)
    up_values = jnp.dot(normed_mlp, up_w, preferred_element_type=jnp.float32)
    activated = (jax.nn.silu(gate_pre) * up_values).astype(jnp.bfloat16)
    unit_part = jnp.dot(activated, down_w, preferred_element_type=jnp.float32)
    result = middle + lax.psum(unit_part, "tensor")
    record = (
        residual_stream,
        inv_attn,
        normed_attn,
        grouped,
        all_keys,
        all_values,
        log_total,
        mixed_heads,
        middle,
        inv_mlp,
        normed_mlp,
        gate_pre,
        up_values,
        activated,
    )
    return (record, result)


def backward_layer(grad_flow, record, params, tables, allowed):
    gain_attn, gain_mlp, query_w, key_w, value_w, out_w, gate_w, up_w, down_w = params
    (
        residual_stream,
        inv_attn,
        normed_attn,
        grouped,
        all_keys,
        all_values,
        log_total,
        mixed_heads,
        middle,
        inv_mlp,
        normed_mlp,
        gate_pre,
        up_values,
        activated,
    ) = record
    cosine, sine_table = tables
    row_count = residual_stream.shape[0]
    query_heads = query_w.shape[1] // HD
    kv_heads = key_w.shape[1] // HD
    down_in = grad_flow.astype(jnp.bfloat16)
    grad_down = jnp.dot(activated.T, down_in, preferred_element_type=jnp.float32)
    hidden_grad = jnp.dot(down_in, down_w.T, preferred_element_type=jnp.float32)
    sigmoid_gate = jax.nn.sigmoid(gate_pre)
    gate_grad = (
        hidden_grad * up_values * sigmoid_gate * (1.0 + gate_pre * (1.0 - sigmoid_gate))
    ).astype(jnp.bfloat16)
    up_grad = (hidden_grad * gate_pre * sigmoid_gate).astype(jnp.bfloat16)
    grad_gate = jnp.dot(normed_mlp.T, gate_grad, preferred_element_type=jnp.float32)
    grad_up = jnp.dot(normed_mlp.T, up_grad, preferred_element_type=jnp.float32)
    unit_back = jnp.dot(gate_grad, gate_w.T, preferred_element_type=jnp.float32) + jnp.dot(
        up_grad, up_w.T, preferred_element_type=jnp.float32
    )
    mlp_norm_grad = lax.psum(unit_back, "tensor")
    middle_grad, grad_gain_mlp = norm_back(middle, inv_mlp, gain_mlp, mlp_norm_grad, grad_flow)
    out_in = middle_grad.astype(jnp.bfloat16)
    grad_out = jnp.dot(mixed_heads.T, out_in, preferred_element_type=jnp.float32)
    mixed_grad = jnp.dot(out_in, out_w.T, preferred_element_type=jnp.float32).astype(jnp.bfloat16)
    mixed_grad = mixed_grad.reshape(row_count, kv_heads, query_heads // kv_heads, HD)
    query_grad, key_grad, value_grad = attention_backward(
        grouped, all_keys, all_values, allowed, log_total, mixed_grad
    )
    key_grad = key_grad.reshape(STRETCHES * row_count, kv_heads * HD)
    value_grad = value_grad.reshape(STRETCHES * row_count, kv_heads * HD)
    key_total = key_grad[:row_count]
    value_total = value_grad[:row_count]
    for distance in range(1, STRETCHES):
        key_piece = key_grad[distance * row_count : (distance + 1) * row_count]
        value_piece = value_grad[distance * row_count : (distance + 1) * row_count]
        moved_keys, moved_values = passed_along((key_piece, value_piece), "dp", -distance)
        key_total = key_total + moved_keys
        value_total = value_total + moved_values
    query_grad = (
        unrotate(query_grad.reshape(row_count, query_heads, HD), cosine, sine_table)
        .astype(jnp.bfloat16)
        .reshape(row_count, query_heads * HD)
    )
    key_total = (
        unrotate(key_total.reshape(row_count, kv_heads, HD), cosine, sine_table)
        .astype(jnp.bfloat16)
        .reshape(row_count, kv_heads * HD)
    )
    value_total = value_total.astype(jnp.bfloat16)
    grad_query = jnp.dot(normed_attn.T, query_grad, preferred_element_type=jnp.float32)
    grad_key = jnp.dot(normed_attn.T, key_total, preferred_element_type=jnp.float32)
    grad_value = jnp.dot(normed_attn.T, value_total, preferred_element_type=jnp.float32)
    head_back = jnp.dot(query_grad, query_w.T, preferred_element_type=jnp.float32)
    head_back = head_back + jnp.dot(key_total, key_w.T, preferred_element_type=jnp.float32)
    head_back = head_back + jnp.dot(value_total, value_w.T, preferred_element_type=jnp.float32)
    attn_norm_grad = lax.psum(head_back, "tensor")
    residual_gradient, grad_gain_attn = norm_back(
        residual_stream, inv_attn, gain_attn, attn_norm_grad, middle_grad
    )
    return (
        residual_gradient,
        (
            grad_gain_attn,
            grad_gain_mlp,
            grad_query,
            grad_key,
            grad_value,
            grad_out,
            grad_gate,
            grad_up,
            grad_down,
        ),
    )


def shards(
    hidden_in,
    doc_lengths,
    norm_attn,
    norm_mlp,
    w_query,
    w_key,
    w_value,
    w_out,
    w_gate,
    w_up,
    w_down,
    cotangent,
):
    row_count = hidden_in.shape[0]
    seq_count = lax.axis_size("dp") // STRETCHES
    shifted_index = lax.axis_index("dp") + STRETCHES // 2
    stretch_index = shifted_index % STRETCHES
    seq_index = shifted_index // STRETCHES % seq_count
    lengths = lax.dynamic_slice_in_dim(doc_lengths, seq_index, 1, 0)
    local_rows = jnp.arange(row_count, dtype=jnp.int32)
    query_place = stretch_index * row_count + local_rows
    query_doc, query_pos = doc_place(query_place, lengths)
    key_parts = []
    for distance in range(STRETCHES):
        key_parts.append((stretch_index - distance) * row_count + local_rows)
    key_place = jnp.concatenate(key_parts)
    key_doc = doc_place(key_place, lengths)[0]
    allowed = (
        (key_place[None, :] >= 0)
        & (key_place[None, :] <= query_place[:, None])
        & (key_doc[None, :] == query_doc[:, None])
    )
    tables = rope_tables(query_pos)
    records = []
    flowing = hidden_in
    for layer_index in range(LAYERS):
        params = (
            norm_attn[layer_index],
            norm_mlp[layer_index],
            w_query[layer_index],
            w_key[layer_index],
            w_value[layer_index],
            w_out[layer_index],
            w_gate[layer_index],
            w_up[layer_index],
            w_down[layer_index],
        )
        record, flowing = forward_layer(flowing, params, tables, allowed)
        records.append(record)
    grad_flow = cotangent
    collected = [None] * LAYERS
    for layer_index in reversed(range(LAYERS)):
        params = (
            norm_attn[layer_index],
            norm_mlp[layer_index],
            w_query[layer_index],
            w_key[layer_index],
            w_value[layer_index],
            w_out[layer_index],
            w_gate[layer_index],
            w_up[layer_index],
            w_down[layer_index],
        )
        grad_flow, layer_grads = backward_layer(
            grad_flow, records[layer_index], params, tables, allowed
        )
        collected[layer_index] = layer_grads
    stacked = tuple(
        (jnp.stack([member[position] for member in collected]) for position in range(9))
    )
    stacked = (
        lax.psum_scatter(
            stacked[0].astype(jnp.bfloat16), "dp", scatter_dimension=1, tiled=True
        ).astype(jnp.float32),
        lax.psum_scatter(
            stacked[1].astype(jnp.bfloat16), "dp", scatter_dimension=1, tiled=True
        ).astype(jnp.float32),
        lax.psum_scatter(
            stacked[2].astype(jnp.bfloat16), "dp", scatter_dimension=1, tiled=True
        ).astype(jnp.float32),
        lax.psum_scatter(
            stacked[3].astype(jnp.bfloat16), "dp", scatter_dimension=1, tiled=True
        ).astype(jnp.float32),
        lax.psum_scatter(
            stacked[4].astype(jnp.bfloat16), "dp", scatter_dimension=1, tiled=True
        ).astype(jnp.float32),
        lax.psum_scatter(
            stacked[5].astype(jnp.bfloat16), "dp", scatter_dimension=2, tiled=True
        ).astype(jnp.float32),
        lax.psum_scatter(
            stacked[6].astype(jnp.bfloat16), "dp", scatter_dimension=1, tiled=True
        ).astype(jnp.float32),
        lax.psum_scatter(
            stacked[7].astype(jnp.bfloat16), "dp", scatter_dimension=1, tiled=True
        ).astype(jnp.float32),
        lax.psum_scatter(
            stacked[8].astype(jnp.bfloat16), "dp", scatter_dimension=2, tiled=True
        ).astype(jnp.float32),
    )
    return (
        flowing,
        grad_flow,
        stacked[0],
        stacked[1],
        stacked[2],
        stacked[3],
        stacked[4],
        stacked[5],
        stacked[6],
        stacked[7],
        stacked[8],
    )


def solution(mesh):
    placed = (
        P("dp", None),
        P(),
        P(),
        P(),
        P(None, None, "tensor"),
        P(None, None, "tensor"),
        P(None, None, "tensor"),
        P(None, "tensor", None),
        P(None, None, "tensor"),
        P(None, None, "tensor"),
        P(None, "tensor", None),
        P("dp", None),
    )
    return jax.shard_map(
        shards,
        mesh=mesh,
        in_specs=placed,
        out_specs=(
            P("dp", None),
            P("dp", None),
            P(None, "dp"),
            P(None, "dp"),
            P(None, "dp", "tensor"),
            P(None, "dp", "tensor"),
            P(None, "dp", "tensor"),
            P(None, "tensor", "dp"),
            P(None, "dp", "tensor"),
            P(None, "dp", "tensor"),
            P(None, "tensor", "dp"),
        ),
        check_vma=False,
    )
```

profile of v0, /device:TPU:0, one launch (start us, length us, event | category | flops | bytes accessed | tf_op | source)
XLA Modules:
  0.0 1885.0 jit_solution(11726850413629536480)
XLA Ops:
  38.5 14.9 collective-permute-done.5
  53.4 4.6 fusion.10
  63.8 4.4 convolution_convert_fusion.15
  72.2 64.6 %all-reduce.13.cloned.1.call-done = f32[512,1536]{1,0:T(8,128)} async-done(((f32[512,1536]{1,0:T(8,128)}), f32[512,1536]{1,0:T(8,128)}) %all-reduce.13.cloned.1.call-update) | async-done | bytes 3145744 | tf_op jit(solution)/shard_map/psum | solution.py:131
  140.5 4.5 fusion.38
  155.3 66.3 %all-reduce.15.cloned.1.call-done = f32[512,1536]{1,0:T(8,128)} async-done(((f32[512,1536]{1,0:T(8,128)}), f32[512,1536]{1,0:T(8,128)}) %all-reduce.15.cloned.1.call-update) | async-done | bytes 3145744 | tf_op jit(solution)/shard_map/psum | solution.py:138
  238.2 22.7 %collective-permute-done.11 = bf16[512,192]{0,1:T(8,128)(2,1)S(1)} collective-permute-done((bf16[512,192]{0,1:T(8,128)(2,1)S(1)}, bf16[512,192]{0,1:T(8,128)(2,1)S(1)}, u32[]{:S(2)}, u32[]{:S(2)}) %collective-permute-start.11) | collective-permute-done | bytes 196640 | tf_op jit(solution)/shard_map/ppermute | solution.py:16
  269.7 4.4 convolution_convert_fusion.14
  279.3 64.6 %all-reduce.17.cloned.1.call-done = f32[512,1536]{1,0:T(8,128)} async-done(((f32[512,1536]{1,0:T(8,128)}), f32[512,1536]{1,0:T(8,128)}) %all-reduce.17.cloned.1.call-update) | async-done | bytes 3145744 | tf_op jit(solution)/shard_map/psum | solution.py:131
  347.7 5.6 fusion.23
  365.1 68.7 %all-reduce.19.cloned.1.call-done = f32[512,1536]{1,0:T(8,128)} async-done(((f32[512,1536]{1,0:T(8,128)}), f32[512,1536]{1,0:T(8,128)}) %all-reduce.19.cloned.1.call-update) | async-done | bytes 3145744 | tf_op jit(solution)/shard_map/psum | solution.py:193
  433.7 4.3 multiply_reduce_fusion
  444.3 9.5 convolution_bitcast_fusion.1
  453.8 8.2 fusion.188
  462.0 25.3 %fusion.63 = f32[2048,2,96]{0,2,1:T(8,128)} fusion(bf16[512,2,2,96]{0,3,2,1:T(8,128)(2,1)} %bitcast.491, f32[2,2048,512,2]{2,1,3,0:T(8,128)} %fusion.188, f32[2,2048,512,2]{2,1,3,0:T(8,128)} %copy-done.12, f32[2,2,512]{2,1,0:T(2,128)} %copy-done.94, pred[512,2048]{0,1:T(8,128)(4,1)} %copy-done.25), kind=kOutput, calls=%fused_computation.113 | convolution fusion | flops 851447808 | bytes 36577280 | tf_op jit(solution)/shard_map/kgqt,qkgd->tkd/dot_general | solution.py:83
  487.3 25.1 %fusion.41 = f32[2,96,2,512]{3,1,2,0:T(8,128)} fusion(f32[2,2048,512,2]{2,1,3,0:T(8,128)} %fusion.188, f32[2,2048,512,2]{2,1,3,0:T(8,128)} %copy-done.12, f32[2,2,512]{2,1,0:T(2,128)} %copy-done.94, pred[512,2048]{0,1:T(8,128)(4,1)} %copy-done.25, bf16[512,2,96]{0,2,1:T(8,128)(2,1)} %bitcast.530, bf16[512,2,96]{0,2,1:T(8,128)(2,1)} %bitcast.528, ...), kind=kOutput, calls=%fused_computation.87 | convolution fusion | flops 854593536 | bytes 36184064 | tf_op jit(solution)/shard_map/kgqt,tkd->qkgd/dot_general | solution.py:80
  514.0 4.3 collective-permute-start.15
  525.8 19.0 %collective-permute-done.12 = f32[512,192]{0,1:T(8,128)S(1)} collective-permute-done((f32[512,192]{0,1:T(8,128)S(1)}, f32[512,192]{0,1:T(8,128)S(1)}, u32[]{:S(2)}, u32[]{:S(2)}) %collective-permute-start.12) | collective-permute-done | bytes 393248 | tf_op jit(solution)/shard_map/ppermute | solution.py:16
  547.4 5.8 collective-permute-done.13
  553.2 8.4 collective-permute-done.14
  562.7 6.1 collective-permute-done.17
  571.9 86.6 %all-reduce.21.cloned.1.call-done = f32[512,1536]{1,0:T(8,128)} async-done(((f32[512,1536]{1,0:T(8,128)}), f32[512,1536]{1,0:T(8,128)}) %all-reduce.21.cloned.1.call-update) | async-done | bytes 3145744 | tf_op jit(solution)/shard_map/psum | solution.py:229
  658.6 4.3 multiply_reduce_fusion.2
  666.2 6.6 multiply_convert_fusion.4
  678.5 5.7 fusion.20
  684.1 63.0 %all-reduce.23.cloned.1.call-done = f32[512,1536]{1,0:T(8,128)} async-done(((f32[512,1536]{1,0:T(8,128)}), f32[512,1536]{1,0:T(8,128)}) %all-reduce.23.cloned.1.call-update) | async-done | bytes 3145744 | tf_op jit(solution)/shard_map/psum | solution.py:193
  754.7 9.7 convolution_bitcast_fusion
  764.4 8.1 fusion.189
  772.5 24.6 %fusion.62 = f32[2048,2,96]{0,2,1:T(8,128)} fusion(bf16[512,2,2,96]{0,3,2,1:T(8,128)(2,1)S(1)} %bitcast.489, f32[2,2048,512,2]{2,1,3,0:T(8,128)} %fusion.189, f32[2,2048,512,2]{2,1,3,0:T(8,128)} %copy-done.11, f32[2,2,512]{2,1,0:T(2,128)S(1)} %copy-done.93, pred[512,2048]{0,1:T(8,128)(4,1)S(1)} %copy-done.28), kind=kOutput, calls=%fused_computation.112 | convolution fusion | flops 851447808 | bytes 36577280 | tf_op jit(solution)/shard_map/kgqt,qkgd->tkd/dot_general | solution.py:83
  797.2 23.6 %fusion.44 = f32[2,96,2,512]{3,1,2,0:T(8,128)S(1)} fusion(f32[2,2048,512,2]{2,1,3,0:T(8,128)} %fusion.189, f32[2,2048,512,2]{2,1,3,0:T(8,128)} %copy-done.11, f32[2,2,512]{2,1,0:T(2,128)S(1)} %copy-done.93, pred[512,2048]{0,1:T(8,128)(4,1)S(1)} %copy-done.28, bf16[512,2,96]{0,2,1:T(8,128)(2,1)} %bitcast.14, bf16[512,2,96]{0,2,1:T(8,128)(2,1)} %bitcast.13, ...), kind=kOutput, calls=%fused_computation.90 | convolution fusion | flops 854593536 | bytes 36184064 | tf_op jit(solution)/shard_map/kgqt,tkd->qkgd/dot_general | solution.py:80
  822.6 4.3 collective-permute-start.21
  834.4 19.0 %collective-permute-done.18 = f32[512,192]{0,1:T(8,128)S(1)} collective-permute-done((f32[512,192]{0,1:T(8,128)S(1)}, f32[512,192]{0,1:T(8,128)S(1)}, u32[]{:S(2)}, u32[]{:S(2)}) %collective-permute-start.18) | collective-permute-done | bytes 393248 | tf_op jit(solution)/shard_map/ppermute | solution.py:16
  855.9 5.9 collective-permute-done.19
  861.8 8.4 collective-permute-done.20
  871.3 6.1 collective-permute-done.23
  887.9 4.9 copy.91
  892.7 4.5 reshape.440
  913.4 105.2 %all-reduce.25.cloned.1.call-done = (f32[512,1536]{1,0:T(8,128)}, f32[512,1536]{1,0:T(8,128)}) async-done(((f32[512,1536]{1,0:T(8,128)}, f32[512,1536]{1,0:T(8,128)}), (f32[512,1536]{1,0:T(8,128)}, f32[512,1536]{1,0:T(8,128)})) %all-reduce.25.cloned.1.call-update) | async-done | bytes 6291472 | tf_op jit(solution)/shard_map/psum | solution.py:138
  1037.8 16.4 copy.64
  1058.7 6.8 copy.63
  1086.7 63.9 %reduce-scatter.28.cloned.1.call-done = bf16[192,384]{1,0:T(8,128)(2,1)} async-done(((bf16[1536,384]{1,0:T(8,128)(2,1)}), bf16[192,384]{1,0:T(8,128)(2,1)}) %reduce-scatter.28.cloned.1.call-update) | async-done | bytes 147472
  1152.8 64.8 %reduce-scatter.26.cloned.1.call-done = bf16[192,384]{1,0:T(8,128)(2,1)} async-done(((bf16[1536,384]{1,0:T(8,128)(2,1)}), bf16[192,384]{1,0:T(8,128)(2,1)}) %reduce-scatter.26.cloned.1.call-update) | async-done | bytes 147472
  1219.7 5.2 add.306
  1227.4 54.4 %reduce-scatter.22.cloned.1.call-done = bf16[192,2]{1,0:T(8,128)(2,1)} async-done(((bf16[1536,2]{1,0:T(8,128)(2,1)}), bf16[192,2]{1,0:T(8,128)(2,1)}) %reduce-scatter.22.cloned.1.call-update) | async-done | bytes 784
  1283.3 69.9 %reduce-scatter.16.cloned.1.call-done = bf16[2,192,384]{2,1,0:T(8,128)(2,1)} async-done(((bf16[2,1536,384]{2,1,0:T(8,128)(2,1)}), bf16[2,192,384]{2,1,0:T(8,128)(2,1)}) %reduce-scatter.16.cloned.1.call-update) | async-done | bytes 294928 | tf_op jit(solution)/shard_map/reduce_scatter | solution.py:327
  1355.0 278.8 %all-reduce.27.cloned.1.call-done = (bf16[2,384,1536]{1,0,2:T(2,128)(2,1)}, bf16[2,1024,1536]{1,0,2:T(2,128)(2,1)}) async-done(((bf16[2,384,1536]{1,0,2:T(2,128)(2,1)}, bf16[2,1024,1536]{1,0,2:T(2,128)(2,1)}), (bf16[2,384,1536]{1,0,2:T(2,128)(2,1)}, bf16[2,1024,1536]{1,0,2:T(2,128)(2,1)})) %all-reduce.27.cloned.1.call-update) | async-done | bytes 8650768
  1639.1 115.5 %reduce-scatter.20.cloned.1.call-done = bf16[2,192,1024]{2,1,0:T(8,128)(2,1)} async-done(((bf16[2,1536,1024]{2,1,0:T(8,128)(2,1)}), bf16[2,192,1024]{2,1,0:T(8,128)(2,1)}) %reduce-scatter.20.cloned.1.call-update) | async-done | bytes 786448 | tf_op jit(solution)/shard_map/reduce_scatter | solution.py:342
  1757.1 118.5 %reduce-scatter.18.cloned.1.call-done = bf16[2,192,1024]{2,1,0:T(8,128)(2,1)} async-done(((bf16[2,1536,1024]{2,1,0:T(8,128)(2,1)}), bf16[2,192,1024]{2,1,0:T(8,128)(2,1)}) %reduce-scatter.18.cloned.1.call-update) | async-done | bytes 786448 | tf_op jit(solution)/shard_map/reduce_scatter | solution.py:339
  (479 shorter events, 242.2 us)
Async XLA Ops:
  7.2 129.6 %all-reduce.13.cloned.1.call-start = ((), (), s32[]{:S(2)}) async-start(), calls=%async_computation.7 | async-start | bytes 6291456 | tf_op jit(solution)/shard_map/psum | solution.py:131
  16.8 19.0 %collective-permute-start.3 = (bf16[512,192]{0,1:T(8,128)(2,1)}, bf16[512,192]{0,1:T(8,128)(2,1)}, u32[]{:S(2)}, u32[]{:S(2)}) collective-permute-start(bf16[512,192]{0,1:T(8,128)(2,1)} %bitcast.11), channel_id=1, source_target_pairs={{28,0},{0,4},{4,8},{8,12},{12,16},{16,20},{20,24},{24,28},{29,1},{... | collective-permute-start | bytes 589832 | tf_op jit(solution)/shard_map/ppermute | solution.py:16
  19.7 18.7 collective-permute-start.4
  21.3 32.1 %collective-permute-start.5 = (bf16[512,192]{0,1:T(8,128)(2,1)}, bf16[512,192]{0,1:T(8,128)(2,1)}, u32[]{:S(2)}, u32[]{:S(2)}) collective-permute-start(bf16[512,192]{0,1:T(8,128)(2,1)} %bitcast.11), channel_id=1, source_target_pairs={{20,0},{24,4},{28,8},{0,12},{4,16},{8,20},{12,24},{16,28},{21,1},{... | collective-permute-start | bytes 589832 | tf_op jit(solution)/shard_map/ppermute | solution.py:16
  24.6 37.1 %collective-permute-start = (bf16[512,192]{0,1:T(8,128)(2,1)S(1)}, bf16[512,192]{0,1:T(8,128)(2,1)S(1)}, u32[]{:S(2)}, u32[]{:S(2)}) collective-permute-start(bf16[512,192]{0,1:T(8,128)(2,1)S(1)} %convolution_convert_fusion.19), channel_id=1, source_target_pairs={{28,0},{0,4},{4,8},{8,12},{12,16},{16,20},{20,24},{24,28},{29,1},{... | collective-permute-start | bytes 589832 | tf_op jit(solution)/shard_map/ppermute | solution.py:16
  26.1 35.6 %collective-permute-start.1 = (bf16[512,192]{0,1:T(8,128)(2,1)S(1)}, bf16[512,192]{0,1:T(8,128)(2,1)}, u32[]{:S(2)}, u32[]{:S(2)}) collective-permute-start(bf16[512,192]{0,1:T(8,128)(2,1)S(1)} %convolution_convert_fusion.19), channel_id=1, source_target_pairs={{24,0},{28,4},{0,8},{4,12},{8,16},{12,20},{16,24},{20,28},{25,1},{... | collective-permute-start | bytes 589832 | tf_op jit(solution)/shard_map/ppermute | solution.py:16
  35.6 27.4 %copy-start.25 = (pred[512,2048]{0,1:T(8,128)(4,1)}, pred[512,2048]{0,1:T(8,128)(4,1)S(1)}, u32[]{:S(2)}) copy-start(pred[512,2048]{0,1:T(8,128)(4,1)S(1)} %compare_and_fusion) | copy-start | bytes 3145732
  35.8 25.9 %collective-permute-start.2 = (bf16[512,192]{0,1:T(8,128)(2,1)S(1)}, bf16[512,192]{0,1:T(8,128)(2,1)S(1)}, u32[]{:S(2)}, u32[]{:S(2)}) collective-permute-start(bf16[512,192]{0,1:T(8,128)(2,1)S(1)} %convolution_convert_fusion.19), channel_id=1, source_target_pairs={{20,0},{24,4},{28,8},{0,12},{4,16},{8,20},{12,24},{16,28},{21,1},{... | collective-permute-start | bytes 589832 | tf_op jit(solution)/shard_map/ppermute | solution.py:16
  70.9 150.6 %all-reduce.15.cloned.1.call-start = ((), (), s32[]{:S(2)}) async-start(), calls=%async_computation.8 | async-start | bytes 6291456 | tf_op jit(solution)/shard_map/psum | solution.py:138
  152.9 191.1 %all-reduce.17.cloned.1.call-start = ((), (), s32[]{:S(2)}) async-start(), calls=%async_computation.9 | async-start | bytes 6291456 | tf_op jit(solution)/shard_map/psum | solution.py:131
  226.2 34.7 %copy-start.71 = (bf16[512,2,96]{0,2,1:T(8,128)(2,1)}, bf16[512,2,96]{0,2,1:T(8,128)(2,1)S(1)}, u32[]{:S(2)}) copy-start(bf16[512,2,96]{0,2,1:T(8,128)(2,1)S(1)} %fusion.129) | copy-start | bytes 589828
  226.2 10.7 collective-permute-start.9
  227.8 10.5 collective-permute-start.10
  229.2 31.6 %collective-permute-start.11 = (bf16[512,192]{0,1:T(8,128)(2,1)S(1)}, bf16[512,192]{0,1:T(8,128)(2,1)S(1)}, u32[]{:S(2)}, u32[]{:S(2)}) collective-permute-start(bf16[512,192]{0,1:T(8,128)(2,1)S(1)} %bitcast.506), channel_id=1, source_target_pairs={{20,0},{24,4},{28,8},{0,12},{4,16},{8,20},{12,24},{16,28},{21,1},{... | collective-permute-start | bytes 589832 | tf_op jit(solution)/shard_map/ppermute | solution.py:16
  232.3 35.3 %collective-permute-start.6 = (bf16[512,192]{0,1:T(8,128)(2,1)S(1)}, bf16[512,192]{0,1:T(8,128)(2,1)S(1)}, u32[]{:S(2)}, u32[]{:S(2)}) collective-permute-start(bf16[512,192]{0,1:T(8,128)(2,1)S(1)} %convolution_convert_fusion.18), channel_id=1, source_target_pairs={{28,0},{0,4},{4,8},{8,12},{12,16},{16,20},{20,24},{24,28},{29,1},{... | collective-permute-start | bytes 589832 | tf_op jit(solution)/shard_map/ppermute | solution.py:16
  233.8 33.8 %collective-permute-start.7 = (bf16[512,192]{0,1:T(8,128)(2,1)S(1)}, bf16[512,192]{0,1:T(8,128)(2,1)S(1)}, u32[]{:S(2)}, u32[]{:S(2)}) collective-permute-start(bf16[512,192]{0,1:T(8,128)(2,1)S(1)} %convolution_convert_fusion.18), channel_id=1, source_target_pairs={{24,0},{28,4},{0,8},{4,12},{8,16},{12,20},{16,24},{20,28},{25,1},{... | collective-permute-start | bytes 589832 | tf_op jit(solution)/shard_map/ppermute | solution.py:16
  235.5 28.4 %copy-start.70 = (bf16[512,4,96]{0,2,1:T(8,128)(2,1)}, bf16[512,4,96]{0,2,1:T(8,128)(2,1)S(1)}, u32[]{:S(2)}) copy-start(bf16[512,4,96]{0,2,1:T(8,128)(2,1)S(1)} %fusion.99) | copy-start | bytes 1179652
  236.9 30.8 %collective-permute-start.8 = (bf16[512,192]{0,1:T(8,128)(2,1)S(1)}, bf16[512,192]{0,1:T(8,128)(2,1)S(1)}, u32[]{:S(2)}, u32[]{:S(2)}) collective-permute-start(bf16[512,192]{0,1:T(8,128)(2,1)S(1)} %convolution_convert_fusion.18), channel_id=1, source_target_pairs={{20,0},{24,4},{28,8},{0,12},{4,16},{8,20},{12,24},{16,28},{21,1},{... | collective-permute-start | bytes 589832 | tf_op jit(solution)/shard_map/ppermute | solution.py:16
  278.8 154.9 %all-reduce.19.cloned.1.call-start = ((), (), s32[]{:S(2)}) async-start(), calls=%async_computation.10 | async-start | bytes 6291456 | tf_op jit(solution)/shard_map/psum | solution.py:193
  365.0 293.5 %all-reduce.21.cloned.1.call-start = ((), (), s32[]{:S(2)}) async-start(), calls=%async_computation.11 | async-start | bytes 6291456 | tf_op jit(solution)/shard_map/psum | solution.py:229
  514.0 48.6 %collective-permute-start.15 = (f32[512,192]{0,1:T(8,128)S(1)}, f32[512,192]{0,1:T(8,128)S(1)}, u32[]{:S(2)}, u32[]{:S(2)}) collective-permute-start(f32[512,192]{0,1:T(8,128)S(1)} %bitcast.497), channel_id=1, source_target_pairs={{4,0},{8,4},{12,8},{16,12},{20,16},{24,20},{28,24},{0,28},{5,1},{9... | collective-permute-start | bytes 1179656 | tf_op jit(solution)/shard_map/ppermute | solution.py:16
  518.3 44.4 %collective-permute-start.16 = (f32[512,192]{0,1:T(8,128)S(1)}, f32[512,192]{0,1:T(8,128)S(1)}, u32[]{:S(2)}, u32[]{:S(2)}) collective-permute-start(f32[512,192]{0,1:T(8,128)S(1)} %bitcast.495), channel_id=1, source_target_pairs={{8,0},{12,4},{16,8},{20,12},{24,16},{28,20},{0,24},{4,28},{9,1},{1... | collective-permute-start | bytes 1179656 | tf_op jit(solution)/shard_map/ppermute | solution.py:16
  519.0 25.7 %collective-permute-start.12 = (f32[512,192]{0,1:T(8,128)S(1)}, f32[512,192]{0,1:T(8,128)S(1)}, u32[]{:S(2)}, u32[]{:S(2)}) collective-permute-start(f32[512,192]{0,1:T(8,128)S(1)} %bitcast.502), channel_id=1, source_target_pairs={{4,0},{8,4},{12,8},{16,12},{20,16},{24,20},{28,24},{0,28},{5,1},{9... | collective-permute-start | bytes 1179656 | tf_op jit(solution)/shard_map/ppermute | solution.py:16
  519.6 33.6 %collective-permute-start.13 = (f32[512,192]{0,1:T(8,128)S(1)}, f32[512,192]{0,1:T(8,128)S(1)}, u32[]{:S(2)}, u32[]{:S(2)}) collective-permute-start(f32[512,192]{0,1:T(8,128)S(1)} %bitcast.500), channel_id=1, source_target_pairs={{8,0},{12,4},{16,8},{20,12},{24,16},{28,20},{0,24},{4,28},{9,1},{1... | collective-permute-start | bytes 1179656 | tf_op jit(solution)/shard_map/ppermute | solution.py:16
  520.2 41.4 %collective-permute-start.14 = (f32[512,192]{0,1:T(8,128)S(1)}, f32[512,192]{0,1:T(8,128)S(1)}, u32[]{:S(2)}, u32[]{:S(2)}) collective-permute-start(f32[512,192]{0,1:T(8,128)S(1)} %bitcast.498), channel_id=1, source_target_pairs={{12,0},{16,4},{20,8},{24,12},{28,16},{0,20},{4,24},{8,28},{13,1},{... | collective-permute-start | bytes 1179656 | tf_op jit(solution)/shard_map/ppermute | solution.py:16
  525.8 36.2 %copy-start.38 = (bf16[2,1536,192]{1,2,0:T(8,128)(2,1)S(1)}, bf16[2,1536,192]{1,2,0:T(8,128)(2,1)}, u32[]{:S(2)}) copy-start(bf16[2,1536,192]{1,2,0:T(8,128)(2,1)} %param.17) | copy-start | bytes 3538948
  544.8 24.0 %collective-permute-start.17 = (f32[512,192]{0,1:T(8,128)S(1)}, f32[512,192]{0,1:T(8,128)S(1)}, u32[]{:S(2)}, u32[]{:S(2)}) collective-permute-start(f32[512,192]{0,1:T(8,128)S(1)} %bitcast.493), channel_id=1, source_target_pairs={{12,0},{16,4},{20,8},{24,12},{28,16},{0,20},{4,24},{8,28},{13,1},{... | collective-permute-start | bytes 1179656 | tf_op jit(solution)/shard_map/ppermute | solution.py:16
  571.9 175.2 %all-reduce.23.cloned.1.call-start = ((), (), s32[]{:S(2)}) async-start(), calls=%async_computation.12 | async-start | bytes 6291456 | tf_op jit(solution)/shard_map/psum | solution.py:193
  678.4 340.1 %all-reduce.25.cloned.1.call-start = ((), (), s32[]{:S(2)}) async-start(), calls=%async_computation.20 | async-start | bytes 12582912 | tf_op jit(solution)/shard_map/psum | solution.py:138
  678.5 68.7 %copy-start.82 = (f32[512]{0:T(512)S(1)}, f32[512]{0:T(512)}, u32[]{:S(2)}) copy-start(f32[512]{0:T(512)} %copy-done.81) | copy-start | bytes 6148
  822.6 48.6 %collective-permute-start.21 = (f32[512,192]{0,1:T(8,128)S(1)}, f32[512,192]{0,1:T(8,128)S(1)}, u32[]{:S(2)}, u32[]{:S(2)}) collective-permute-start(f32[512,192]{0,1:T(8,128)S(1)} %bitcast.496), channel_id=1, source_target_pairs={{4,0},{8,4},{12,8},{16,12},{20,16},{24,20},{28,24},{0,28},{5,1},{9... | collective-permute-start | bytes 1179656 | tf_op jit(solution)/shard_map/ppermute | solution.py:16
  826.9 44.4 %collective-permute-start.22 = (f32[512,192]{0,1:T(8,128)S(1)}, f32[512,192]{0,1:T(8,128)S(1)}, u32[]{:S(2)}, u32[]{:S(2)}) collective-permute-start(f32[512,192]{0,1:T(8,128)S(1)} %bitcast.494), channel_id=1, source_target_pairs={{8,0},{12,4},{16,8},{20,12},{24,16},{28,20},{0,24},{4,28},{9,1},{1... | collective-permute-start | bytes 1179656 | tf_op jit(solution)/shard_map/ppermute | solution.py:16
  827.6 25.7 %collective-permute-start.18 = (f32[512,192]{0,1:T(8,128)S(1)}, f32[512,192]{0,1:T(8,128)S(1)}, u32[]{:S(2)}, u32[]{:S(2)}) collective-permute-start(f32[512,192]{0,1:T(8,128)S(1)} %bitcast.503), channel_id=1, source_target_pairs={{4,0},{8,4},{12,8},{16,12},{20,16},{24,20},{28,24},{0,28},{5,1},{9... | collective-permute-start | bytes 1179656 | tf_op jit(solution)/shard_map/ppermute | solution.py:16
  828.2 33.6 %collective-permute-start.19 = (f32[512,192]{0,1:T(8,128)S(1)}, f32[512,192]{0,1:T(8,128)S(1)}, u32[]{:S(2)}, u32[]{:S(2)}) collective-permute-start(f32[512,192]{0,1:T(8,128)S(1)} %bitcast.501), channel_id=1, source_target_pairs={{8,0},{12,4},{16,8},{20,12},{24,16},{28,20},{0,24},{4,28},{9,1},{1... | collective-permute-start | bytes 1179656 | tf_op jit(solution)/shard_map/ppermute | solution.py:16
  828.8 41.4 %collective-permute-start.20 = (f32[512,192]{0,1:T(8,128)S(1)}, f32[512,192]{0,1:T(8,128)S(1)}, u32[]{:S(2)}, u32[]{:S(2)}) collective-permute-start(f32[512,192]{0,1:T(8,128)S(1)} %bitcast.499), channel_id=1, source_target_pairs={{12,0},{16,4},{20,8},{24,12},{28,16},{0,20},{4,24},{8,28},{13,1},{... | collective-permute-start | bytes 1179656 | tf_op jit(solution)/shard_map/ppermute | solution.py:16
  834.4 36.2 %copy-start.39 = (bf16[2,1536,192]{1,2,0:T(8,128)(2,1)S(1)}, bf16[2,1536,192]{1,2,0:T(8,128)(2,1)}, u32[]{:S(2)}) copy-start(bf16[2,1536,192]{1,2,0:T(8,128)(2,1)} %param.17) | copy-start | bytes 3538948
  853.4 24.0 %collective-permute-start.23 = (f32[512,192]{0,1:T(8,128)S(1)}, f32[512,192]{0,1:T(8,128)S(1)}, u32[]{:S(2)}, u32[]{:S(2)}) collective-permute-start(f32[512,192]{0,1:T(8,128)S(1)} %bitcast.492), channel_id=1, source_target_pairs={{12,0},{16,4},{20,8},{24,12},{28,16},{0,20},{4,24},{8,28},{13,1},{... | collective-permute-start | bytes 1179656 | tf_op jit(solution)/shard_map/ppermute | solution.py:16
  880.5 204.7 %reduce-scatter.24.cloned.1.call-start = ((), (), s32[]{:S(2)}) async-start(), calls=%async_computation.17 | async-start | bytes 442368
  884.2 266.5 %reduce-scatter.28.cloned.1.call-start = ((), (), s32[]{:S(2)}) async-start(), calls=%async_computation.19 | async-start | bytes 1327104
  897.3 320.3 %reduce-scatter.26.cloned.1.call-start = ((), (), s32[]{:S(2)}) async-start(), calls=%async_computation.18 | async-start | bytes 1327104
  905.8 376.0 %reduce-scatter.22.cloned.1.call-start = ((), (), s32[]{:S(2)}) async-start(), calls=%async_computation.16 | async-start | bytes 442368
  907.7 110.8 %copy-start.3 = (f32[512,1536]{1,0:T(8,128)S(1)}, f32[512,1536]{1,0:T(8,128)}, u32[]{:S(2)}) copy-start(f32[512,1536]{1,0:T(8,128)} %param.12) | copy-start | bytes 9437188
  907.7 110.8 %copy-start.73 = (f32[1536]{0:T(1024)S(1)}, f32[1536]{0:T(1024)}, u32[]{:S(2)}) copy-start(f32[1536]{0:T(1024)} %copy-done.72) | copy-start | bytes 18436
  907.7 110.8 %copy-start.80 = (f32[512]{0:T(512)S(1)}, f32[512]{0:T(512)}, u32[]{:S(2)}) copy-start(f32[512]{0:T(512)} %copy-done.79) | copy-start | bytes 6148
  1022.2 331.0 %reduce-scatter.16.cloned.1.call-start = ((), (), s32[]{:S(2)}) async-start(), calls=%async_computation.13 | async-start | bytes 2654208 | tf_op jit(solution)/shard_map/reduce_scatter | solution.py:327
  1025.6 608.2 %all-reduce.27.cloned.1.call-start = ((), (), s32[]{:S(2)}) async-start(), calls=%async_computation.21 | async-start | bytes 17301504
  1065.5 689.1 %reduce-scatter.20.cloned.1.call-start = ((), (), s32[]{:S(2)}) async-start(), calls=%async_computation.15 | async-start | bytes 7077888 | tf_op jit(solution)/shard_map/reduce_scatter | solution.py:342
  1074.3 801.3 %reduce-scatter.18.cloned.1.call-start = ((), (), s32[]{:S(2)}) async-start(), calls=%async_computation.14 | async-start | bytes 7077888 | tf_op jit(solution)/shard_map/reduce_scatter | solution.py:339
  (117 other events, 633.8 us)
Sparse Core Ops, SparseCore 0:
  71.1 65.7 all-reduce.12
  153.0 68.5 all-reduce.14
  278.9 64.9 all-reduce.16
  365.1 68.5 all-reduce.18
  572.0 86.5 all-reduce.20
  678.5 68.5 all-reduce.22
  880.6 137.8 all-reduce.24
  1022.4 61.5 reduce-scatter.23
  1087.4 63.2 reduce-scatter.27
  1154.5 63.0 reduce-scatter.25
  1221.4 60.3 reduce-scatter.21
  1285.1 68.0 reduce-scatter.15
  1357.2 276.5 all-reduce.26
  1637.7 116.9 reduce-scatter.19
  1758.5 117.0 reduce-scatter.17
where the time goes:
time: 1890 us; the launch traced here: 1880 us
  waiting for transfers between devices  1400 us (74%)
  matrix products  249 us (13%)
  other arithmetic  89 us (5%)
  local copies, waits for them, and re-layouts  81.4 us (4%)
  starting transfers between devices  45.7 us (2%)
    unnamed x20, waiting for transfers between devices  462 us
    psum x2, waiting for transfers between devices, forward_layer(): result = middle + lax.psum(unit_part, 'tensor')  171 us
    psum x2, waiting for transfers between devices, backward_layer(): mlp_norm_grad = lax.psum(unit_back, 'tensor')  132 us
    psum x2, waiting for transfers between devices, forward_layer(): middle = residual_stream + lax.psum(head_part, 'tensor')  129 us
    reduce_scatter x1, waiting for transfers between devices, shards(): lax.psum_scatter(stacked[6].astype(jnp.bfloat16), 'dp', scatter_dimension...  119 us
    ppermute x24, waiting for transfers between devices, passed_along(): return lax.ppermute(block, axis, route)  118 us
    reduce_scatter x1, waiting for transfers between devices, shards(): lax.psum_scatter(stacked[7].astype(jnp.bfloat16), 'dp', scatter_dimension...  116 us
    psum x1, waiting for transfers between devices, backward_layer(): attn_norm_grad = lax.psum(head_back, 'tensor')  86.6 us
  transfers between devices with their start and end apart: 39, of which 25 were waited for; matrix products, arithmetic and copies ran while one was open for 9% of the time, Pallas kernels for 0%

commit v1 on v0

--- a/solution.py
+++ b/solution.py
@@ -190,7 +190,11 @@
     unit_back = jnp.dot(gate_grad, gate_w.T, preferred_element_type=jnp.float32) + jnp.dot(
         up_grad, up_w.T, preferred_element_type=jnp.float32
     )
-    mlp_norm_grad = lax.psum(unit_back, "tensor")
+    mlp_norm_grad = unit_back
+    for hop in (1, 2):
+        mlp_norm_grad = mlp_norm_grad + lax.ppermute(
+            mlp_norm_grad, "tensor", [(dev, dev ^ hop) for dev in range(4)]
+        )
     middle_grad, grad_gain_mlp = norm_back(middle, inv_mlp, gain_mlp, mlp_norm_grad, grad_flow)
     out_in = middle_grad.astype(jnp.bfloat16)
     grad_out = jnp.dot(mixed_heads.T, out_in, preferred_element_type=jnp.float32)

time: 1890 us -> 1900 us (level)
    ppermute x0 -> x4, waiting for transfers between devices: none -> 147 us  [backward_layer(): lax.ppermute(mlp_norm_grad, 'tensor', [(dev, dev ^ hop) for dev in range(...]
    psum x2 -> x0, waiting for transfers between devices: 132 us -> none  [backward_layer(): mlp_norm_grad = lax.psum(unit_back, 'tensor')]
    unnamed x269 -> x257, local copies, waits for them, and re-layouts: 43.1 us -> 44.5 us
    unnamed x20 -> x18, waiting for transfers between devices: 462 us -> 461 us
  transfers between devices with their start and end apart: 39 -> 41, of which waited for: 25 -> 27; matrix products, arithmetic and copies ran while one was open for 9% -> 8% of each run, Pallas kernels for 0% -> 0%
where the time goes in v1:
time: 1900 us; the launch traced here: 1890 us
  waiting for transfers between devices  1410 us (74%)
  matrix products  247 us (13%)
  local copies, waits for them, and re-layouts  83.8 us (4%)
  other arithmetic  81.1 us (4%)
  starting transfers between devices  46.8 us (2%)
    unnamed x18, waiting for transfers between devices  461 us
    psum x2, waiting for transfers between devices, forward_layer(): result = middle + lax.psum(unit_part, 'tensor')  171 us
    ppermute x4, waiting for transfers between devices, backward_layer(): lax.ppermute(mlp_norm_grad, 'tensor', [(dev, dev ^ hop) for dev in range(...  147 us
    psum x2, waiting for transfers between devices, forward_layer(): middle = residual_stream + lax.psum(head_part, 'tensor')  129 us
    reduce_scatter x1, waiting for transfers between devices, shards(): lax.psum_scatter(stacked[7].astype(jnp.bfloat16), 'dp', scatter_dimension...  119 us
    reduce_scatter x1, waiting for transfers between devices, shards(): lax.psum_scatter(stacked[6].astype(jnp.bfloat16), 'dp', scatter_dimension...  118 us
    ppermute x24, waiting for transfers between devices, passed_along(): return lax.ppermute(block, axis, route)  113 us
    psum x1, waiting for transfers between devices, backward_layer(): attn_norm_grad = lax.psum(head_back, 'tensor')  86.4 us
  transfers between devices with their start and end apart: 41, of which 27 were waited for; matrix products, arithmetic and copies ran while one was open for 8% of the time, Pallas kernels for 0%

profile of v1, /device:TPU:0, one launch (start us, length us, event | category | flops | bytes accessed | tf_op | source)
XLA Modules:
  0.0 1890.3 jit_solution(13806280222664640690)
XLA Ops:
  42.1 11.3 collective-permute-done.5
  53.3 4.6 fusion.10
  63.9 4.4 convolution_convert_fusion.15
  74.9 63.9 %all-reduce.11.cloned.1.call-done = f32[512,1536]{1,0:T(8,128)} async-done(((f32[512,1536]{1,0:T(8,128)}), f32[512,1536]{1,0:T(8,128)}) %all-reduce.11.cloned.1.call-update) | async-done | bytes 3145744 | tf_op jit(solution)/shard_map/psum | solution.py:131
  141.6 5.6 fusion.38
  157.7 66.0 %all-reduce.13.cloned.1.call-done = f32[512,1536]{1,0:T(8,128)} async-done(((f32[512,1536]{1,0:T(8,128)}), f32[512,1536]{1,0:T(8,128)}) %all-reduce.13.cloned.1.call-update) | async-done | bytes 3145744 | tf_op jit(solution)/shard_map/psum | solution.py:138
  240.6 22.9 %collective-permute-done.11 = bf16[512,192]{0,1:T(8,128)(2,1)S(1)} collective-permute-done((bf16[512,192]{0,1:T(8,128)(2,1)S(1)}, bf16[512,192]{0,1:T(8,128)(2,1)S(1)}, u32[]{:S(2)}, u32[]{:S(2)}) %collective-permute-start.11) | collective-permute-done | bytes 196640 | tf_op jit(solution)/shard_map/ppermute | solution.py:16
  272.4 4.4 convolution_convert_fusion.14
  281.7 64.9 %all-reduce.15.cloned.1.call-done = f32[512,1536]{1,0:T(8,128)} async-done(((f32[512,1536]{1,0:T(8,128)}), f32[512,1536]{1,0:T(8,128)}) %all-reduce.15.cloned.1.call-update) | async-done | bytes 3145744 | tf_op jit(solution)/shard_map/psum | solution.py:131
  349.3 5.6 fusion.23
  356.8 5.8 multiply_convert_fusion.6
  366.5 5.6 collective-permute-done.12
  373.2 69.7 %collective-permute-done.13 = f32[512,1536]{1,0:T(8,128)S(1)} collective-permute-done((f32[512,1536]{1,0:T(8,128)S(1)}, f32[512,1536]{1,0:T(8,128)S(1)}, u32[]{:S(2)}, u32[]{:S(2)}) %collective-permute-start.13) | collective-permute-done | bytes 3145760 | tf_op jit(solution)/shard_map/ppermute | solution.py:195
  448.3 9.5 convolution_bitcast_fusion.1
  457.9 8.2 fusion.188
  466.1 25.2 %fusion.63 = f32[2048,2,96]{0,2,1:T(8,128)} fusion(bf16[512,2,2,96]{0,3,2,1:T(8,128)(2,1)} %bitcast.491, f32[2,2048,512,2]{2,1,3,0:T(8,128)} %fusion.188, f32[2,2048,512,2]{2,1,3,0:T(8,128)} %copy-done.11, f32[2,2,512]{2,1,0:T(2,128)S(1)} %copy-done.87, pred[512,2048]{0,1:T(8,128)(4,1)} %copy-done.21), kind=kOutput, calls=%fused_computation.113 | convolution fusion | flops 851447808 | bytes 36577280 | tf_op jit(solution)/shard_map/kgqt,qkgd->tkd/dot_general | solution.py:83
  491.3 25.1 %fusion.41 = f32[2,96,2,512]{3,1,2,0:T(8,128)} fusion(f32[2,2048,512,2]{2,1,3,0:T(8,128)} %fusion.188, f32[2,2048,512,2]{2,1,3,0:T(8,128)} %copy-done.11, f32[2,2,512]{2,1,0:T(2,128)S(1)} %copy-done.87, pred[512,2048]{0,1:T(8,128)(4,1)} %copy-done.21, bf16[512,2,96]{0,2,1:T(8,128)(2,1)} %bitcast.530, bf16[512,2,96]{0,2,1:T(8,128)(2,1)} %bitcast.528, ...), kind=kOutput, calls=%fused_computation.87 | convolution fusion | flops 854593536 | bytes 36184064 | tf_op jit(solution)/shard_map/kgqt,tkd->qkgd/dot_general | solution.py:80
  518.1 4.3 collective-permute-start.17
  529.8 19.0 %collective-permute-done.14 = f32[512,192]{0,1:T(8,128)S(1)} collective-permute-done((f32[512,192]{0,1:T(8,128)S(1)}, f32[512,192]{0,1:T(8,128)S(1)}, u32[]{:S(2)}, u32[]{:S(2)}) %collective-permute-start.14) | collective-permute-done | bytes 393248 | tf_op jit(solution)/shard_map/ppermute | solution.py:16
  551.7 5.6 collective-permute-done.15
  557.2 8.4 collective-permute-done.16
  566.7 5.6 collective-permute-done.19
  575.5 86.4 %all-reduce.17.cloned.1.call-done = f32[512,1536]{1,0:T(8,128)} async-done(((f32[512,1536]{1,0:T(8,128)}), f32[512,1536]{1,0:T(8,128)}) %all-reduce.17.cloned.1.call-update) | async-done | bytes 3145744 | tf_op jit(solution)/shard_map/psum | solution.py:233
  668.9 4.7 multiply_convert_fusion.4
  677.6 5.6 collective-permute-done.20
  687.8 66.2 %collective-permute-done.21 = f32[512,1536]{1,0:T(8,128)S(1)} collective-permute-done((f32[512,1536]{1,0:T(8,128)S(1)}, f32[512,1536]{1,0:T(8,128)S(1)}, u32[]{:S(2)}, u32[]{:S(2)}) %collective-permute-start.21) | collective-permute-done | bytes 3145760 | tf_op jit(solution)/shard_map/ppermute | solution.py:195
  758.9 9.5 convolution_bitcast_fusion
  768.4 8.1 fusion.189
  776.5 24.6 %fusion.62 = f32[2048,2,96]{0,2,1:T(8,128)} fusion(bf16[512,2,2,96]{0,3,2,1:T(8,128)(2,1)S(1)} %bitcast.489, f32[2,2048,512,2]{2,1,3,0:T(8,128)} %fusion.189, f32[2,2048,512,2]{2,1,3,0:T(8,128)} %copy-done.10, f32[2,2,512]{2,1,0:T(2,128)S(1)} %copy-done.85, pred[512,2048]{0,1:T(8,128)(4,1)S(1)} %copy-done.24), kind=kOutput, calls=%fused_computation.112 | convolution fusion | flops 851447808 | bytes 36577280 | tf_op jit(solution)/shard_map/kgqt,qkgd->tkd/dot_general | solution.py:83
  801.2 23.6 %fusion.44 = f32[2,96,2,512]{3,1,2,0:T(8,128)S(1)} fusion(f32[2,2048,512,2]{2,1,3,0:T(8,128)} %fusion.189, f32[2,2048,512,2]{2,1,3,0:T(8,128)} %copy-done.10, f32[2,2,512]{2,1,0:T(2,128)S(1)} %copy-done.85, pred[512,2048]{0,1:T(8,128)(4,1)S(1)} %copy-done.24, bf16[512,2,96]{0,2,1:T(8,128)(2,1)} %bitcast.14, bf16[512,2,96]{0,2,1:T(8,128)(2,1)} %bitcast.13, ...), kind=kOutput, calls=%fused_computation.90 | convolution fusion | flops 854593536 | bytes 36184064 | tf_op jit(solution)/shard_map/kgqt,tkd->qkgd/dot_general | solution.py:80
  826.6 4.3 collective-permute-start.25
  838.4 19.0 %collective-permute-done.22 = f32[512,192]{0,1:T(8,128)S(1)} collective-permute-done((f32[512,192]{0,1:T(8,128)S(1)}, f32[512,192]{0,1:T(8,128)S(1)}, u32[]{:S(2)}, u32[]{:S(2)}) %collective-permute-start.22) | collective-permute-done | bytes 393248 | tf_op jit(solution)/shard_map/ppermute | solution.py:16
  860.0 5.8 collective-permute-done.23
  865.8 8.4 collective-permute-done.24
  875.3 5.6 collective-permute-done.27
  891.5 4.9 copy.91
  896.3 4.5 reshape.440
  917.0 104.9 %all-reduce.19.cloned.1.call-done = (f32[512,1536]{1,0:T(8,128)}, f32[512,1536]{1,0:T(8,128)}) async-done(((f32[512,1536]{1,0:T(8,128)}, f32[512,1536]{1,0:T(8,128)}), (f32[512,1536]{1,0:T(8,128)}, f32[512,1536]{1,0:T(8,128)})) %all-reduce.19.cloned.1.call-update) | async-done | bytes 6291472 | tf_op jit(solution)/shard_map/psum | solution.py:138
  1059.2 16.4 copy.64
  1080.0 6.8 copy.63
  1090.2 63.6 %reduce-scatter.28.cloned.1.call-done = bf16[192,384]{1,0:T(8,128)(2,1)} async-done(((bf16[1536,384]{1,0:T(8,128)(2,1)}), bf16[192,384]{1,0:T(8,128)(2,1)}) %reduce-scatter.28.cloned.1.call-update) | async-done | bytes 147472
  1155.9 64.9 %reduce-scatter.26.cloned.1.call-done = bf16[192,384]{1,0:T(8,128)(2,1)} async-done(((bf16[1536,384]{1,0:T(8,128)(2,1)}), bf16[192,384]{1,0:T(8,128)(2,1)}) %reduce-scatter.26.cloned.1.call-update) | async-done | bytes 147472
  1222.9 5.2 add.314
  1230.7 54.4 %reduce-scatter.22.cloned.1.call-done = bf16[192,2]{1,0:T(8,128)(2,1)} async-done(((bf16[1536,2]{1,0:T(8,128)(2,1)}), bf16[192,2]{1,0:T(8,128)(2,1)}) %reduce-scatter.22.cloned.1.call-update) | async-done | bytes 784
  1286.5 69.9 %reduce-scatter.16.cloned.1.call-done = bf16[2,192,384]{2,1,0:T(8,128)(2,1)} async-done(((bf16[2,1536,384]{2,1,0:T(8,128)(2,1)}), bf16[2,192,384]{2,1,0:T(8,128)(2,1)}) %reduce-scatter.16.cloned.1.call-update) | async-done | bytes 294928 | tf_op jit(solution)/shard_map/reduce_scatter | solution.py:331
  1358.2 118.9 %reduce-scatter.20.cloned.1.call-done = bf16[2,192,1024]{2,1,0:T(8,128)(2,1)} async-done(((bf16[2,1536,1024]{2,1,0:T(8,128)(2,1)}), bf16[2,192,1024]{2,1,0:T(8,128)(2,1)}) %reduce-scatter.20.cloned.1.call-update) | async-done | bytes 786448 | tf_op jit(solution)/shard_map/reduce_scatter | solution.py:346
  1479.5 118.1 %reduce-scatter.18.cloned.1.call-done = bf16[2,192,1024]{2,1,0:T(8,128)(2,1)} async-done(((bf16[2,1536,1024]{2,1,0:T(8,128)(2,1)}), bf16[2,192,1024]{2,1,0:T(8,128)(2,1)}) %reduce-scatter.18.cloned.1.call-update) | async-done | bytes 786448 | tf_op jit(solution)/shard_map/reduce_scatter | solution.py:343
  1600.1 278.1 %all-reduce.21.cloned.1.call-done = (bf16[2,384,1536]{1,0,2:T(2,128)(2,1)}, bf16[2,1024,1536]{1,0,2:T(2,128)(2,1)}) async-done(((bf16[2,384,1536]{1,0,2:T(2,128)(2,1)}, bf16[2,1024,1536]{1,0,2:T(2,128)(2,1)}), (bf16[2,384,1536]{1,0,2:T(2,128)(2,1)}, bf16[2,1024,1536]{1,0,2:T(2,128)(2,1)})) %all-reduce.21.cloned.1.call-update) | async-done | bytes 8650768
  (471 shorter events, 245.3 us)
Async XLA Ops:
  7.2 131.7 %all-reduce.11.cloned.1.call-start = ((), (), s32[]{:S(2)}) async-start(), calls=%async_computation.7 | async-start | bytes 6291456 | tf_op jit(solution)/shard_map/psum | solution.py:131
  16.8 22.7 %collective-permute-start.3 = (bf16[512,192]{0,1:T(8,128)(2,1)}, bf16[512,192]{0,1:T(8,128)(2,1)}, u32[]{:S(2)}, u32[]{:S(2)}) collective-permute-start(bf16[512,192]{0,1:T(8,128)(2,1)} %bitcast.11), channel_id=1, source_target_pairs={{28,0},{0,4},{4,8},{8,12},{12,16},{16,20},{20,24},{24,28},{29,1},{... | collective-permute-start | bytes 589832 | tf_op jit(solution)/shard_map/ppermute | solution.py:16
  19.7 22.4 %collective-permute-start.4 = (bf16[512,192]{0,1:T(8,128)(2,1)}, bf16[512,192]{0,1:T(8,128)(2,1)}, u32[]{:S(2)}, u32[]{:S(2)}) collective-permute-start(bf16[512,192]{0,1:T(8,128)(2,1)} %bitcast.11), channel_id=1, source_target_pairs={{24,0},{28,4},{0,8},{4,12},{8,16},{12,20},{16,24},{20,28},{25,1},{... | collective-permute-start | bytes 589832 | tf_op jit(solution)/shard_map/ppermute | solution.py:16
  21.3 32.0 %collective-permute-start.5 = (bf16[512,192]{0,1:T(8,128)(2,1)}, bf16[512,192]{0,1:T(8,128)(2,1)}, u32[]{:S(2)}, u32[]{:S(2)}) collective-permute-start(bf16[512,192]{0,1:T(8,128)(2,1)} %bitcast.11), channel_id=1, source_target_pairs={{20,0},{24,4},{28,8},{0,12},{4,16},{8,20},{12,24},{16,28},{21,1},{... | collective-permute-start | bytes 589832 | tf_op jit(solution)/shard_map/ppermute | solution.py:16
  25.2 36.5 %collective-permute-start = (bf16[512,192]{0,1:T(8,128)(2,1)}, bf16[512,192]{0,1:T(8,128)(2,1)}, u32[]{:S(2)}, u32[]{:S(2)}) collective-permute-start(bf16[512,192]{0,1:T(8,128)(2,1)} %convolution_convert_fusion.19), channel_id=1, source_target_pairs={{28,0},{0,4},{4,8},{8,12},{12,16},{16,20},{20,24},{24,28},{29,1},{... | collective-permute-start | bytes 589832 | tf_op jit(solution)/shard_map/ppermute | solution.py:16
  26.7 35.0 %collective-permute-start.1 = (bf16[512,192]{0,1:T(8,128)(2,1)}, bf16[512,192]{0,1:T(8,128)(2,1)}, u32[]{:S(2)}, u32[]{:S(2)}) collective-permute-start(bf16[512,192]{0,1:T(8,128)(2,1)} %convolution_convert_fusion.19), channel_id=1, source_target_pairs={{24,0},{28,4},{0,8},{4,12},{8,16},{12,20},{16,24},{20,28},{25,1},{... | collective-permute-start | bytes 589832 | tf_op jit(solution)/shard_map/ppermute | solution.py:16
  39.5 22.2 %collective-permute-start.2 = (bf16[512,192]{0,1:T(8,128)(2,1)}, bf16[512,192]{0,1:T(8,128)(2,1)S(1)}, u32[]{:S(2)}, u32[]{:S(2)}) collective-permute-start(bf16[512,192]{0,1:T(8,128)(2,1)} %convolution_convert_fusion.19), channel_id=1, source_target_pairs={{20,0},{24,4},{28,8},{0,12},{4,16},{8,20},{12,24},{16,28},{21,1},{... | collective-permute-start | bytes 589832 | tf_op jit(solution)/shard_map/ppermute | solution.py:16
  73.0 150.7 %all-reduce.13.cloned.1.call-start = ((), (), s32[]{:S(2)}) async-start(), calls=%async_computation.8 | async-start | bytes 6291456 | tf_op jit(solution)/shard_map/psum | solution.py:138
  155.0 191.6 %all-reduce.15.cloned.1.call-start = ((), (), s32[]{:S(2)}) async-start(), calls=%async_computation.9 | async-start | bytes 6291456 | tf_op jit(solution)/shard_map/psum | solution.py:131
  228.9 10.7 collective-permute-start.9
  230.4 10.2 collective-permute-start.10
  231.9 31.6 %collective-permute-start.11 = (bf16[512,192]{0,1:T(8,128)(2,1)S(1)}, bf16[512,192]{0,1:T(8,128)(2,1)S(1)}, u32[]{:S(2)}, u32[]{:S(2)}) collective-permute-start(bf16[512,192]{0,1:T(8,128)(2,1)S(1)} %bitcast.506), channel_id=1, source_target_pairs={{20,0},{24,4},{28,8},{0,12},{4,16},{8,20},{12,24},{16,28},{21,1},{... | collective-permute-start | bytes 589832 | tf_op jit(solution)/shard_map/ppermute | solution.py:16
  235.0 35.3 %collective-permute-start.6 = (bf16[512,192]{0,1:T(8,128)(2,1)S(1)}, bf16[512,192]{0,1:T(8,128)(2,1)S(1)}, u32[]{:S(2)}, u32[]{:S(2)}) collective-permute-start(bf16[512,192]{0,1:T(8,128)(2,1)S(1)} %convolution_convert_fusion.18), channel_id=1, source_target_pairs={{28,0},{0,4},{4,8},{8,12},{12,16},{16,20},{20,24},{24,28},{29,1},{... | collective-permute-start | bytes 589832 | tf_op jit(solution)/shard_map/ppermute | solution.py:16
  236.5 33.8 %collective-permute-start.7 = (bf16[512,192]{0,1:T(8,128)(2,1)S(1)}, bf16[512,192]{0,1:T(8,128)(2,1)S(1)}, u32[]{:S(2)}, u32[]{:S(2)}) collective-permute-start(bf16[512,192]{0,1:T(8,128)(2,1)S(1)} %convolution_convert_fusion.18), channel_id=1, source_target_pairs={{24,0},{28,4},{0,8},{4,12},{8,16},{12,20},{16,24},{20,28},{25,1},{... | collective-permute-start | bytes 589832 | tf_op jit(solution)/shard_map/ppermute | solution.py:16
  239.5 30.8 %collective-permute-start.8 = (bf16[512,192]{0,1:T(8,128)(2,1)S(1)}, bf16[512,192]{0,1:T(8,128)(2,1)S(1)}, u32[]{:S(2)}, u32[]{:S(2)}) collective-permute-start(bf16[512,192]{0,1:T(8,128)(2,1)S(1)} %convolution_convert_fusion.18), channel_id=1, source_target_pairs={{20,0},{24,4},{28,8},{0,12},{4,16},{8,20},{12,24},{16,28},{21,1},{... | collective-permute-start | bytes 589832 | tf_op jit(solution)/shard_map/ppermute | solution.py:16
  281.5 380.4 %all-reduce.17.cloned.1.call-start = ((), (), s32[]{:S(2)}) async-start(), calls=%async_computation.10 | async-start | bytes 6291456 | tf_op jit(solution)/shard_map/psum | solution.py:233
  348.9 95.6 %copy-start.4 = (f32[512,1536]{1,0:T(8,128)}, f32[512,1536]{1,0:T(8,128)S(1)}, u32[]{:S(2)}) copy-start(f32[512,1536]{1,0:T(8,128)S(1)} %get-tuple-element.63) | copy-start | bytes 9437188
  366.4 5.7 collective-permute-start.12
  372.7 70.2 %collective-permute-start.13 = (f32[512,1536]{1,0:T(8,128)S(1)}, f32[512,1536]{1,0:T(8,128)S(1)}, u32[]{:S(2)}, u32[]{:S(2)}) collective-permute-start(f32[512,1536]{1,0:T(8,128)S(1)} %add.317), channel_id=1, source_target_pairs={{0,2},{1,3},{2,0},{3,1},{4,6},{5,7},{6,4},{7,5},{8,10},{9,11},{10,... | collective-permute-start | bytes 9437192 | tf_op jit(solution)/shard_map/ppermute | solution.py:195
  518.1 48.7 %collective-permute-start.17 = (f32[512,192]{0,1:T(8,128)S(1)}, f32[512,192]{0,1:T(8,128)S(1)}, u32[]{:S(2)}, u32[]{:S(2)}) collective-permute-start(f32[512,192]{0,1:T(8,128)S(1)} %bitcast.497), channel_id=1, source_target_pairs={{4,0},{8,4},{12,8},{16,12},{20,16},{24,20},{28,24},{0,28},{5,1},{9... | collective-permute-start | bytes 1179656 | tf_op jit(solution)/shard_map/ppermute | solution.py:16
  522.3 44.4 %collective-permute-start.18 = (f32[512,192]{0,1:T(8,128)S(1)}, f32[512,192]{0,1:T(8,128)S(1)}, u32[]{:S(2)}, u32[]{:S(2)}) collective-permute-start(f32[512,192]{0,1:T(8,128)S(1)} %bitcast.495), channel_id=1, source_target_pairs={{8,0},{12,4},{16,8},{20,12},{24,16},{28,20},{0,24},{4,28},{9,1},{1... | collective-permute-start | bytes 1179656 | tf_op jit(solution)/shard_map/ppermute | solution.py:16
  523.0 25.8 %collective-permute-start.14 = (f32[512,192]{0,1:T(8,128)S(1)}, f32[512,192]{0,1:T(8,128)S(1)}, u32[]{:S(2)}, u32[]{:S(2)}) collective-permute-start(f32[512,192]{0,1:T(8,128)S(1)} %bitcast.502), channel_id=1, source_target_pairs={{4,0},{8,4},{12,8},{16,12},{20,16},{24,20},{28,24},{0,28},{5,1},{9... | collective-permute-start | bytes 1179656 | tf_op jit(solution)/shard_map/ppermute | solution.py:16
  523.7 33.6 %collective-permute-start.15 = (f32[512,192]{0,1:T(8,128)S(1)}, f32[512,192]{0,1:T(8,128)S(1)}, u32[]{:S(2)}, u32[]{:S(2)}) collective-permute-start(f32[512,192]{0,1:T(8,128)S(1)} %bitcast.500), channel_id=1, source_target_pairs={{8,0},{12,4},{16,8},{20,12},{24,16},{28,20},{0,24},{4,28},{9,1},{1... | collective-permute-start | bytes 1179656 | tf_op jit(solution)/shard_map/ppermute | solution.py:16
  524.2 41.5 %collective-permute-start.16 = (f32[512,192]{0,1:T(8,128)S(1)}, f32[512,192]{0,1:T(8,128)S(1)}, u32[]{:S(2)}, u32[]{:S(2)}) collective-permute-start(f32[512,192]{0,1:T(8,128)S(1)} %bitcast.498), channel_id=1, source_target_pairs={{12,0},{16,4},{20,8},{24,12},{28,16},{0,20},{4,24},{8,28},{13,1},{... | collective-permute-start | bytes 1179656 | tf_op jit(solution)/shard_map/ppermute | solution.py:16
  548.8 23.6 %collective-permute-start.19 = (f32[512,192]{0,1:T(8,128)S(1)}, f32[512,192]{0,1:T(8,128)S(1)}, u32[]{:S(2)}, u32[]{:S(2)}) collective-permute-start(f32[512,192]{0,1:T(8,128)S(1)} %bitcast.493), channel_id=1, source_target_pairs={{12,0},{16,4},{20,8},{24,12},{28,16},{0,20},{4,24},{8,28},{13,1},{... | collective-permute-start | bytes 1179656 | tf_op jit(solution)/shard_map/ppermute | solution.py:16
  575.4 86.5 %copy-start.80 = (f32[512]{0:T(512)S(1)}, f32[512]{0:T(512)}, u32[]{:S(2)}) copy-start(f32[512]{0:T(512)} %copy-done.79) | copy-start | bytes 6148
  575.5 446.4 %all-reduce.19.cloned.1.call-start = ((), (), s32[]{:S(2)}) async-start(), calls=%async_computation.18 | async-start | bytes 12582912 | tf_op jit(solution)/shard_map/psum | solution.py:138
  666.6 88.4 %copy-start.19 = (f32[512,1536]{1,0:T(8,128)}, f32[512,1536]{1,0:T(8,128)S(1)}, u32[]{:S(2)}) copy-start(f32[512,1536]{1,0:T(8,128)S(1)} %multiply_add_fusion.2) | copy-start | bytes 9437188
  677.5 5.7 collective-permute-start.20
  683.8 70.2 %collective-permute-start.21 = (f32[512,1536]{1,0:T(8,128)S(1)}, f32[512,1536]{1,0:T(8,128)S(1)}, u32[]{:S(2)}, u32[]{:S(2)}) collective-permute-start(f32[512,1536]{1,0:T(8,128)S(1)} %add.333), channel_id=1, source_target_pairs={{0,2},{1,3},{2,0},{3,1},{4,6},{5,7},{6,4},{7,5},{8,10},{9,11},{10,... | collective-permute-start | bytes 9437192 | tf_op jit(solution)/shard_map/ppermute | solution.py:195
  684.3 69.7 %copy-start.3 = (f32[512,1536]{1,0:T(8,128)S(1)}, f32[512,1536]{1,0:T(8,128)}, u32[]{:S(2)}) copy-start(f32[512,1536]{1,0:T(8,128)} %copy-done.2) | copy-start | bytes 9437188
  826.6 48.7 %collective-permute-start.25 = (f32[512,192]{0,1:T(8,128)S(1)}, f32[512,192]{0,1:T(8,128)S(1)}, u32[]{:S(2)}, u32[]{:S(2)}) collective-permute-start(f32[512,192]{0,1:T(8,128)S(1)} %bitcast.496), channel_id=1, source_target_pairs={{4,0},{8,4},{12,8},{16,12},{20,16},{24,20},{28,24},{0,28},{5,1},{9... | collective-permute-start | bytes 1179656 | tf_op jit(solution)/shard_map/ppermute | solution.py:16
  830.9 44.4 %collective-permute-start.26 = (f32[512,192]{0,1:T(8,128)S(1)}, f32[512,192]{0,1:T(8,128)S(1)}, u32[]{:S(2)}, u32[]{:S(2)}) collective-permute-start(f32[512,192]{0,1:T(8,128)S(1)} %bitcast.494), channel_id=1, source_target_pairs={{8,0},{12,4},{16,8},{20,12},{24,16},{28,20},{0,24},{4,28},{9,1},{1... | collective-permute-start | bytes 1179656 | tf_op jit(solution)/shard_map/ppermute | solution.py:16
  831.6 25.8 %collective-permute-start.22 = (f32[512,192]{0,1:T(8,128)S(1)}, f32[512,192]{0,1:T(8,128)S(1)}, u32[]{:S(2)}, u32[]{:S(2)}) collective-permute-start(f32[512,192]{0,1:T(8,128)S(1)} %bitcast.503), channel_id=1, source_target_pairs={{4,0},{8,4},{12,8},{16,12},{20,16},{24,20},{28,24},{0,28},{5,1},{9... | collective-permute-start | bytes 1179656 | tf_op jit(solution)/shard_map/ppermute | solution.py:16
  832.2 33.6 %collective-permute-start.23 = (f32[512,192]{0,1:T(8,128)S(1)}, f32[512,192]{0,1:T(8,128)S(1)}, u32[]{:S(2)}, u32[]{:S(2)}) collective-permute-start(f32[512,192]{0,1:T(8,128)S(1)} %bitcast.501), channel_id=1, source_target_pairs={{8,0},{12,4},{16,8},{20,12},{24,16},{28,20},{0,24},{4,28},{9,1},{1... | collective-permute-start | bytes 1179656 | tf_op jit(solution)/shard_map/ppermute | solution.py:16
  832.8 41.5 %collective-permute-start.24 = (f32[512,192]{0,1:T(8,128)S(1)}, f32[512,192]{0,1:T(8,128)S(1)}, u32[]{:S(2)}, u32[]{:S(2)}) collective-permute-start(f32[512,192]{0,1:T(8,128)S(1)} %bitcast.499), channel_id=1, source_target_pairs={{12,0},{16,4},{20,8},{24,12},{28,16},{0,20},{4,24},{8,28},{13,1},{... | collective-permute-start | bytes 1179656 | tf_op jit(solution)/shard_map/ppermute | solution.py:16
  857.4 23.6 %collective-permute-start.27 = (f32[512,192]{0,1:T(8,128)S(1)}, f32[512,192]{0,1:T(8,128)S(1)}, u32[]{:S(2)}, u32[]{:S(2)}) collective-permute-start(f32[512,192]{0,1:T(8,128)S(1)} %bitcast.492), channel_id=1, source_target_pairs={{12,0},{16,4},{20,8},{24,12},{28,16},{0,20},{4,24},{8,28},{13,1},{... | collective-permute-start | bytes 1179656 | tf_op jit(solution)/shard_map/ppermute | solution.py:16
  884.1 204.6 %reduce-scatter.24.cloned.1.call-start = ((), (), s32[]{:S(2)}) async-start(), calls=%async_computation.15 | async-start | bytes 442368
  887.8 266.0 %reduce-scatter.28.cloned.1.call-start = ((), (), s32[]{:S(2)}) async-start(), calls=%async_computation.17 | async-start | bytes 1327104
  900.9 319.9 %reduce-scatter.26.cloned.1.call-start = ((), (), s32[]{:S(2)}) async-start(), calls=%async_computation.16 | async-start | bytes 1327104
  909.4 375.6 %reduce-scatter.22.cloned.1.call-start = ((), (), s32[]{:S(2)}) async-start(), calls=%async_computation.14 | async-start | bytes 442368
  911.3 110.6 %copy-start.1 = (f32[512,1536]{1,0:T(8,128)S(1)}, f32[512,1536]{1,0:T(8,128)}, u32[]{:S(2)}) copy-start(f32[512,1536]{1,0:T(8,128)} %param.12) | copy-start | bytes 9437188
  911.3 110.6 %copy-start.69 = (f32[1536]{0:T(1024)S(1)}, f32[1536]{0:T(1024)}, u32[]{:S(2)}) copy-start(f32[1536]{0:T(1024)} %copy-done.68) | copy-start | bytes 18436
  911.4 110.6 %copy-start.76 = (f32[512]{0:T(512)S(1)}, f32[512]{0:T(512)}, u32[]{:S(2)}) copy-start(f32[512]{0:T(512)} %copy-done.75) | copy-start | bytes 6148
  1025.6 330.8 %reduce-scatter.16.cloned.1.call-start = ((), (), s32[]{:S(2)}) async-start(), calls=%async_computation.11 | async-start | bytes 2654208 | tf_op jit(solution)/shard_map/reduce_scatter | solution.py:331
  1029.0 448.1 %reduce-scatter.20.cloned.1.call-start = ((), (), s32[]{:S(2)}) async-start(), calls=%async_computation.13 | async-start | bytes 7077888 | tf_op jit(solution)/shard_map/reduce_scatter | solution.py:346
  1038.1 559.5 %reduce-scatter.18.cloned.1.call-start = ((), (), s32[]{:S(2)}) async-start(), calls=%async_computation.12 | async-start | bytes 7077888 | tf_op jit(solution)/shard_map/reduce_scatter | solution.py:343
  1047.0 831.2 %all-reduce.21.cloned.1.call-start = ((), (), s32[]{:S(2)}) async-start(), calls=%async_computation.19 | async-start | bytes 17301504
  (113 other events, 997.0 us)
Sparse Core Ops, SparseCore 0:
  73.1 65.7 all-reduce.10
  155.1 68.5 all-reduce.12
  281.6 64.9 all-reduce.14
  575.6 86.2 all-reduce.16
  884.2 137.6 all-reduce.18
  1025.6 61.5 reduce-scatter.23
  1090.5 63.2 reduce-scatter.27
  1157.8 62.9 reduce-scatter.25
  1224.7 60.3 reduce-scatter.21
  1288.4 68.0 reduce-scatter.15
  1360.0 117.0 reduce-scatter.19
  1480.5 117.0 reduce-scatter.17
  1601.7 276.5 all-reduce.20
